TPU v7x, 32 devices: a whole 2x2x4 slice. The times are simulated.
32 devices in a mesh: expert: 4 (over y, core), dp: 8 (over z, x).
Axes of the slice: x: 2, y: 2, z: 4, core: 2. Of those that a mesh axis runs over, the one named last changes fastest.
Arguments:
- tokens: bfloat16 [2048, 3584], P(('dp', 'expert')), parts along dimension 0, may hold values from -6 to 6
- expert_ids: int32 [2048, 1], P(('dp', 'expert')), parts along dimension 0, may hold values from 0 to 3; in each aligned block of 64 rows (0 to 63, 64 to 127, ...) at most 18 rows name the same one
- combine: bfloat16 [2048, 1], P(('dp', 'expert')), parts along dimension 0, may hold values from 0.19921875 to 1
- w_gate: bfloat16 [3584, 8192], P(None, 'expert'), may hold values from -0.09375 to 0.09375
- w_up: bfloat16 [3584, 8192], P(None, 'expert'), may hold values from -0.09375 to 0.09375
- w_down: bfloat16 [8192, 3584], P('expert'), may hold values from -0.125 to 0.125
Outputs:
- mixed: bfloat16 [2048, 3584], P(('dp', 'expert')), parts along dimension 0
There are 8 independent parts, one for each index of `dp`. A program takes and returns all parts, laid end to end along the dimension named above; an argument that names none is the same for every part. Nothing has to cross between parts.
Inputs may be any that keep to these rules, and one draw needn't show every extreme that they name: `expert_ids`: each token names one expert. Among the 64 tokens of one device (aligned blocks of rows) no expert is named more than 18 times, a bound that some block reaches.
All inputs are finite; a program needn't handle non-finite values.
Results may differ from a plain program's by a relative error of at most 0.0057.
Values may be sent and summed in bfloat16 or wider, within the bound.
A program may use at most 128 MiB of HBM per device.

v0:
```python
import jax
import jax.numpy as jnp
from jax import lax
from jax.sharding import PartitionSpec as P

EXPERTS = 4
TOP = 1
CAP = 18


def local(tokens, expert_ids, combine, w_gate, w_up, w_down):
    devices = lax.axis_size("expert")
    span_size = devices // EXPERTS
    model_width = tokens.shape[1]
    token_count = tokens.shape[0]
    flat_ids = expert_ids.reshape(-1)
    labels = jnp.arange(EXPERTS, dtype=jnp.int32)
    member = (flat_ids[:, None] == labels[None, :]).astype(jnp.int32)
    rank_table = jnp.cumsum(member, axis=0) - 1
    positions = jnp.sum(member * rank_table, axis=1)
    slot_ids = jnp.arange(CAP, dtype=jnp.int32)
    placed = (member.T[:, None, :] == 1) & (positions[None, None, :] == slot_ids[None, :, None])
    repeated = jnp.repeat(tokens, TOP, axis=0)
    outgoing = jnp.einsum(
        "ecf,fd->ecd", placed.astype(jnp.bfloat16), repeated, preferred_element_type=jnp.float32
    ).astype(jnp.bfloat16)
    outgoing = jnp.repeat(outgoing, span_size, axis=0)
    arrived = lax.all_to_all(outgoing, "expert", split_axis=0, concat_axis=0, tiled=True)
    slot_count = arrived.shape[1]
    row_block = arrived.reshape(-1, model_width)
    gate_values = jnp.dot(row_block, w_gate, preferred_element_type=jnp.float32)
    up_values = jnp.dot(row_block, w_up, preferred_element_type=jnp.float32)
    hidden = (jax.nn.silu(gate_values) * up_values).astype(jnp.bfloat16)
    result = (
        jnp.dot(hidden, w_down, preferred_element_type=jnp.float32)
        .astype(jnp.bfloat16)
        .reshape(devices, slot_count, model_width)
    )
    returned_rows = lax.all_to_all(result, "expert", split_axis=0, concat_axis=0, tiled=True)
    summed = jnp.sum(
        returned_rows.astype(jnp.float32).reshape(EXPERTS, span_size, CAP, model_width), axis=1
    )
    weighted = placed.astype(jnp.float32) * combine.astype(jnp.float32).reshape(-1)[None, None, :]
    entry_rows = jnp.einsum("ecf,ecd->fd", weighted, summed, precision=lax.Precision.HIGHEST)
    mixed_rows = jnp.sum(entry_rows.reshape(token_count, TOP, model_width), axis=1)
    return mixed_rows.astype(jnp.bfloat16)


def solution(mesh):
    placed = (
        P(("dp", "expert"), None),
        P(("dp", "expert"), None),
        P(("dp", "expert"), None),
        P(None, "expert"),
        P(None, "expert"),
        P("expert", None),
    )
    return jax.shard_map(
        local, mesh=mesh, in_specs=placed, out_specs=P(("dp", "expert"), None), check_vma=False
    )
```

profile of v0, /device:TPU:0, one launch (start us, length us, event | category | flops | bytes accessed | tf_op | source)
XLA Modules:
  0.0 56.4 jit_solution(2965514269756863854)
XLA Ops:
  0.0 0.0 copy-start
  0.0 0.8 %fusion.5 = s32[64,4]{1,0:T(8,128)S(1)} fusion(s32[64]{0:T(128)} %bitcast.17), kind=kLoop, calls=%fused_computation.12 | loop fusion | flops 512 | bytes 1280 | tf_op jit(solution)/shard_map/convert_element_type | solution.py:18
  0.8 0.7 %convert_compare_fusion = pred[4,64]{1,0:T(4,128)(4,1)S(1)} fusion(s32[64]{0:T(128)} %bitcast.18), kind=kLoop, calls=%fused_computation.20 | loop fusion | flops 768 | bytes 512 | tf_op jit(solution)/shard_map/eq | solution.py:22
  1.4 0.1 reduce_window_sum.11
  1.5 0.8 %select_reduce_fusion = s32[64]{0:T(128)S(1)} fusion(s32[64,4]{1,0:T(8,128)S(1)} %reduce_window_sum.11, s32[64]{0:T(128)} %bitcast.19), kind=kLoop, calls=%fused_computation.10 | loop fusion | flops 960 | bytes 1536 | tf_op jit(solution)/shard_map/reduce_sum | solution.py:20
  2.4 0.0 copy-done
  2.4 0.3 convolution_convert_fusion
  2.7 14.6 %all_to_all.10 = bf16[4,18,3584]{2,1,0:T(8,128)(2,1)S(1)} all-to-all(bf16[4,18,3584]{2,1,0:T(8,128)(2,1)S(1)} %convolution_convert_fusion), channel_id=1, replica_groups=mesh['expert'=4,'dp'=8] {'expert'}, dimensions={0} | all-to-all | bytes 1032192 | tf_op jit(solution)/shard_map/all_to_all | solution.py:28
  17.4 0.2 reshape.60
  17.5 7.8 %fusion.14 = f32[72,2048]{1,0:T(8,128)S(1)} fusion(bf16[72,3584]{1,0:T(8,128)(2,1)S(1)} %reshape.60, bf16[3584,2048]{1,0:T(8,128)(2,1)} %param.9), kind=kOutput, calls=%fused_computation.25 | convolution fusion | flops 1056964608 | bytes 15785984 | tf_op jit(solution)/shard_map/dot_general | solution.py:31
  25.4 0.0 copy-start.1
  25.4 14.6 %convolution_convert_fusion.1 = bf16[72,3584]{1,0:T(8,128)(2,1)S(1)} fusion(bf16[2048,3584]{1,0:T(8,128)(2,1)} %param.11, bf16[72,3584]{1,0:T(8,128)(2,1)S(1)} %reshape.60, bf16[3584,2048]{1,0:T(8,128)(2,1)} %param.10, f32[72,2048]{1,0:T(8,128)S(1)} %fusion.14), kind=kOutput, calls=%fused_computation.2 | convolution fusion | flops 2115072000 | bytes 30982144 | tf_op jit(solution)/shard_map/dot_general | solution.py:35
  40.0 1.0 %reshape.61 = bf16[4,18,3584]{2,1,0:T(8,128)(2,1)} reshape(bf16[72,3584]{1,0:T(8,128)(2,1)S(1)} %convolution_convert_fusion.1) | data formatting | bytes 1032192 | tf_op jit(solution)/shard_map/reshape | solution.py:37
  41.0 3.5 %all-to-all-start.1 = ((bf16[4,18,3584]{2,1,0:T(8,128)(2,1)}), bf16[4,18,3584]{2,1,0:T(8,128)(2,1)S(1)}, u32[]{:S(2)}, u32[]{:S(2)}) async-start(bf16[4,18,3584]{2,1,0:T(8,128)(2,1)} %reshape.61), calls=%async_computation.1 | async-start | bytes 1376256 | tf_op jit(solution)/shard_map/all_to_all | solution.py:39
  44.5 0.0 copy-done.1
  44.5 10.5 %all-to-all-done.1 = bf16[4,18,3584]{2,1,0:T(8,128)(2,1)S(1)} async-done(((bf16[4,18,3584]{2,1,0:T(8,128)(2,1)}), bf16[4,18,3584]{2,1,0:T(8,128)(2,1)S(1)}, u32[]{:S(2)}, u32[]{:S(2)}) %all-to-all-start.1) | async-done | bytes 516128 | tf_op jit(solution)/shard_map/all_to_all | solution.py:39
  55.0 1.4 %fusion = bf16[64,3584]{1,0:T(8,128)(2,1)} fusion(bf16[4,18,3584]{2,1,0:T(8,128)(2,1)S(1)} %all-to-all-done.1, f32[64]{0:T(128)S(1)} %bitcast_convert_fusion, pred[18,64]{1,0:T(8,128)(4,1)S(1)} %iota_compare_fusion.1, pred[4,64]{1,0:T(4,128)(4,1)S(1)} %convert_compare_fusion), kind=kOutput, calls=%fused_computation.3 | convolution fusion | flops 198419456 | bytes 976512 | tf_op jit(solution)/shard_map/ecf,ecd->fd/dot_general | solution.py:44
  (2 shorter events, 0.0 us)
Async XLA Ops:
  0.0 2.4 %copy-start = (bf16[64,3584]{1,0:T(8,128)(2,1)S(1)}, bf16[64,3584]{1,0:T(8,128)(2,1)}, u32[]{:S(2)}) copy-start(bf16[64,3584]{1,0:T(8,128)(2,1)} %param.6) | copy-start | bytes 1376260
  25.4 19.1 %copy-start.1 = (bf16[64,1]{0,1:T(2,128)(2,1)S(1)}, bf16[64,1]{0,1:T(2,128)(2,1)}, u32[]{:S(2)}) copy-start(bf16[64,1]{0,1:T(2,128)(2,1)} %param.8) | copy-start | bytes 388
  41.0 14.0 %all-to-all-start.1 = ((bf16[4,18,3584]{2,1,0:T(8,128)(2,1)}), bf16[4,18,3584]{2,1,0:T(8,128)(2,1)S(1)}, u32[]{:S(2)}, u32[]{:S(2)}) async-start(bf16[4,18,3584]{2,1,0:T(8,128)(2,1)} %reshape.61), calls=%async_computation.1 | async-start | bytes 1376256 | tf_op jit(solution)/shard_map/all_to_all | solution.py:39
where the time goes:
time: 56.7 us; the launch traced here: 56.4 us
  matrix products  24.1 us (43%)
  blocking collectives  14.6 us (26%)
  waiting for transfers between devices  10.5 us (19%)
  starting transfers between devices  3.48 us (6%)
  other arithmetic  2.38 us (4%)
  local copies, waits for them, and re-layouts  1.19 us (2%)
    all_to_all x1, blocking collectives, local(): lax.all_to_all(outgoing, 'expert', split_axis=0, concat_axis=0, tiled=True)  14.6 us
    dot_general x1, matrix products, local(): jnp.dot(hidden, w_down, preferred_element_type=jnp.float32)  14.6 us
    all_to_all x1, waiting for transfers between devices, local(): lax.all_to_all(result, 'expert', split_axis=0, concat_axis=0, tiled=True)  10.5 us
    dot_general x1, matrix products, local(): gate_values = jnp.dot(row_block, w_gate, preferred_element_type=jnp.float32)  7.85 us
    all_to_all x1, starting transfers between devices, local(): lax.all_to_all(result, 'expert', split_axis=0, concat_axis=0, tiled=True)  3.48 us
    dot_general x1, matrix products, local(): jnp.einsum('ecf,ecd->fd', weighted, summed, precision=lax.Precision.HIGHEST)  1.35 us
  transfers between devices with their start and end apart: 1, of which 1 were waited for; matrix products, arithmetic and copies ran while one was open for 0% of the time, Pallas kernels for 0%

commit v1 on v0

--- a/solution.py
+++ b/solution.py
@@ -1,3 +1,4 @@
+import functools
 import jax
 import jax.numpy as jnp
 from jax import lax
@@ -6,6 +7,36 @@
 EXPERTS = 4
 TOP = 1
 CAP = 18
+
+
+def feed_tables_on_mesh(own_rows, where_dim, mine_x):
+    res, moved = (own_rows.shape[:where_dim], own_rows.shape[where_dim + 1 :])
+    return jnp.moveaxis(own_rows.reshape(*res, mine_x, -1, *moved), where_dim, 0)
+
+
+def _get_waves(a0, at_axis):
+    a0 = jnp.moveaxis(a0, 0, at_axis)
+    met_up = a0.shape
+    return a0.reshape(
+        *met_up[:at_axis], met_up[at_axis] * met_up[at_axis + 1], *met_up[at_axis + 2 :]
+    )
+
+
+def change_bench(view, axis_tag, inputs, tile_in):
+    all_rows = lax.axis_size(axis_tag)
+    fresh, extra = (all_rows, lax.axis_index(axis_tag))
+    w2 = feed_tables_on_mesh(view, inputs, fresh)
+    heap = [w2[extra]]
+    for w in range(1, fresh):
+        v_now = w2[extra ^ w]
+        heap.append(
+            lax.ppermute(v_now, axis_name=axis_tag, perm=[(it, it ^ w) for it in range(fresh)])
+        )
+    w2 = jnp.stack(heap, axis=0)[extra ^ jnp.arange(fresh)]
+    return _get_waves(w2, tile_in)
+
+
+hold_positions = functools.partial(change_bench, axis_tag="expert", inputs=0, tile_in=0)
 
 
 def local(tokens, expert_ids, combine, w_gate, w_up, w_down):
@@ -25,7 +56,7 @@
         "ecf,fd->ecd", placed.astype(jnp.bfloat16), repeated, preferred_element_type=jnp.float32
     ).astype(jnp.bfloat16)
     outgoing = jnp.repeat(outgoing, span_size, axis=0)
-    arrived = lax.all_to_all(outgoing, "expert", split_axis=0, concat_axis=0, tiled=True)
+    arrived = hold_positions(outgoing)
     slot_count = arrived.shape[1]
     row_block = arrived.reshape(-1, model_width)
     gate_values = jnp.dot(row_block, w_gate, preferred_element_type=jnp.float32)

time: 56.7 us -> 54.3 us (0.958)
  blocking collectives: 14.6 us -> 0 us
  waiting for transfers between devices: 10.5 us -> 18.8 us
  starting transfers between devices: 3.48 us -> 6.66 us
  local copies, waits for them, and re-layouts: 1.19 us -> 1.87 us
    all_to_all x1 -> x0, blocking collectives: 14.6 us -> none  [local(): lax.all_to_all(outgoing, 'expert', split_axis=0, concat_axis=0, tiled=True)]
    ppermute x0 -> x3, waiting for transfers between devices: none -> 8.33 us  [change_bench(): lax.ppermute(v_now, axis_name=axis_tag, perm=[(it, it ^ w) for it in rang...]
    ppermute x0 -> x3, starting transfers between devices: none -> 3.17 us  [change_bench(): lax.ppermute(v_now, axis_name=axis_tag, perm=[(it, it ^ w) for it in rang...]
    gather x0 -> x1, local copies, waits for them, and re-layouts: none -> 0.59 us  [change_bench(): w2 = jnp.stack(heap, axis=0)[extra ^ jnp.arange(fresh)]]
  transfers between devices with their start and end apart: 1 -> 4, of which waited for: 1 -> 3; matrix products, arithmetic and copies ran while one was open for 0% -> 0% of each run, Pallas kernels for 0% -> 0%
where the time goes in v1:
time: 54.3 us; the launch traced here: 54.1 us
  matrix products  24.1 us (44%)
  waiting for transfers between devices  18.8 us (35%)
  starting transfers between devices  6.66 us (12%)
  other arithmetic  2.5 us (5%)
  local copies, waits for them, and re-layouts  1.87 us (3%)
    dot_general x1, matrix products, local(): jnp.dot(hidden, w_down, preferred_element_type=jnp.float32)  14.6 us
    all_to_all x1, waiting for transfers between devices, local(): lax.all_to_all(result, 'expert', split_axis=0, concat_axis=0, tiled=True)  10.5 us
    ppermute x3, waiting for transfers between devices, change_bench(): lax.ppermute(v_now, axis_name=axis_tag, perm=[(it, it ^ w) for it in rang...  8.33 us
    dot_general x1, matrix products, local(): gate_values = jnp.dot(row_block, w_gate, preferred_element_type=jnp.float32)  7.84 us
    all_to_all x1, starting transfers between devices, local(): lax.all_to_all(result, 'expert', split_axis=0, concat_axis=0, tiled=True)  3.48 us
    ppermute x3, starting transfers between devices, change_bench(): lax.ppermute(v_now, axis_name=axis_tag, perm=[(it, it ^ w) for it in rang...  3.17 us
    dot_general x1, matrix products, local(): jnp.einsum('ecf,ecd->fd', weighted, summed, precision=lax.Precision.HIGHEST)  1.35 us
  transfers between devices with their start and end apart: 4, of which 3 were waited for; matrix products, arithmetic and copies ran while one was open for 0% of the time, Pallas kernels for 0%

profile of v1, /device:TPU:0, one launch (start us, length us, event | category | flops | bytes accessed | tf_op | source)
XLA Modules:
  0.0 54.1 jit_solution(15778936134714178556)
XLA Ops:
  0.0 0.0 copy-start
  0.0 0.8 %fusion.5 = s32[64,4]{1,0:T(8,128)S(1)} fusion(s32[64]{0:T(128)} %bitcast.29), kind=kLoop, calls=%fused_computation.15 | loop fusion | flops 512 | bytes 1280 | tf_op jit(solution)/shard_map/convert_element_type | solution.py:49
  0.8 0.7 %convert_compare_fusion = pred[4,64]{1,0:T(4,128)(4,1)S(1)} fusion(s32[64]{0:T(128)} %bitcast.30), kind=kLoop, calls=%fused_computation.25 | loop fusion | flops 768 | bytes 512 | tf_op jit(solution)/shard_map/eq | solution.py:53
  1.4 0.1 reduce_window_sum.11
  1.5 0.8 %select_reduce_fusion = s32[64]{0:T(128)S(1)} fusion(s32[64,4]{1,0:T(8,128)S(1)} %reduce_window_sum.11, s32[64]{0:T(128)} %bitcast.31), kind=kLoop, calls=%fused_computation.13 | loop fusion | flops 960 | bytes 1536 | tf_op jit(solution)/shard_map/reduce_sum | solution.py:51
  2.4 0.0 copy-done
  2.4 0.3 convolution_convert_fusion
  2.7 0.1 dynamic-slice_bitcast_fusion
  2.8 0.6 %collective-permute-start = (bf16[1,18,3584]{2,1,0:T(8,128)(2,1)S(1)}, bf16[1,18,3584]{2,1,0:T(8,128)(2,1)S(1)}, u32[]{:S(2)}, u32[]{:S(2)}) collective-permute-start(bf16[1,18,3584]{2,1,0:T(8,128)(2,1)S(1)} %get-tuple-element.8), channel_id=1, source_target_pairs={{0,8},{8,0},{16,24},{24,16},{1,9},{9,1},{17,25},{25,17},{2,10},{10... | collective-permute-start | bytes 387080 | tf_op jit(solution)/shard_map/ppermute | solution.py:33
  3.4 2.6 %collective-permute-start.1 = (bf16[1,18,3584]{2,1,0:T(8,128)(2,1)S(1)}, bf16[1,18,3584]{2,1,0:T(8,128)(2,1)S(1)}, u32[]{:S(2)}, u32[]{:S(2)}) collective-permute-start(bf16[1,18,3584]{2,1,0:T(8,128)(2,1)S(1)} %get-tuple-element.7), channel_id=1, source_target_pairs={{0,16},{8,24},{16,0},{24,8},{1,17},{9,25},{17,1},{25,9},{2,18},{10... | collective-permute-start | bytes 387080 | tf_op jit(solution)/shard_map/ppermute | solution.py:33
  6.0 0.0 collective-permute-start.2
  6.0 0.0 collective-permute-done
  6.0 5.2 %collective-permute-done.1 = bf16[1,18,3584]{2,1,0:T(8,128)(2,1)S(1)} collective-permute-done((bf16[1,18,3584]{2,1,0:T(8,128)(2,1)S(1)}, bf16[1,18,3584]{2,1,0:T(8,128)(2,1)S(1)}, u32[]{:S(2)}, u32[]{:S(2)}) %collective-permute-start.1) | collective-permute-done | bytes 129056 | tf_op jit(solution)/shard_map/ppermute | solution.py:33
  11.2 3.2 %collective-permute-done.2 = bf16[1,18,3584]{2,1,0:T(8,128)(2,1)S(1)} collective-permute-done((bf16[1,18,3584]{2,1,0:T(8,128)(2,1)S(1)}, bf16[1,18,3584]{2,1,0:T(8,128)(2,1)S(1)}, u32[]{:S(2)}, u32[]{:S(2)}) %collective-permute-start.2) | collective-permute-done | bytes 129056 | tf_op jit(solution)/shard_map/ppermute | solution.py:33
  14.4 0.1 maximum_bitcast_fusion
  14.5 0.6 %gather_fusion = bf16[4,18,3584]{2,1,0:T(8,128)(2,1)S(1)} fusion(bf16[4,18,3584]{2,1,0:T(8,128)(2,1)S(1)} %maximum_bitcast_fusion, s32[1024]{0:T(1024)S(1)} %pad_clamp_fusion), kind=kCustom, calls=%fused_computation | custom fusion | bytes 1032208 | tf_op jit(solution)/shard_map/gather | solution.py:35
  15.1 0.2 reshape_reshape.3
  15.2 7.8 %fusion.15 = f32[72,2048]{1,0:T(8,128)S(1)} fusion(bf16[72,3584]{1,0:T(8,128)(2,1)S(1)} %reshape_reshape.3, bf16[3584,2048]{1,0:T(8,128)(2,1)} %param.9), kind=kOutput, calls=%fused_computation.34 | convolution fusion | flops 1056964608 | bytes 15785984 | tf_op jit(solution)/shard_map/dot_general | solution.py:62
  23.1 0.0 copy-start.1
  23.1 14.6 %convolution_convert_fusion.1 = bf16[72,3584]{1,0:T(8,128)(2,1)S(1)} fusion(bf16[2048,3584]{1,0:T(8,128)(2,1)} %param.11, bf16[72,3584]{1,0:T(8,128)(2,1)S(1)} %reshape_reshape.3, bf16[3584,2048]{1,0:T(8,128)(2,1)} %param.10, f32[72,2048]{1,0:T(8,128)S(1)} %fusion.15), kind=kOutput, calls=%fused_computation.3 | convolution fusion | flops 2115072000 | bytes 30982144 | tf_op jit(solution)/shard_map/dot_general | solution.py:66
  37.7 1.0 %reshape.80 = bf16[4,18,3584]{2,1,0:T(8,128)(2,1)} reshape(bf16[72,3584]{1,0:T(8,128)(2,1)S(1)} %convolution_convert_fusion.1) | data formatting | bytes 1032192 | tf_op jit(solution)/shard_map/reshape | solution.py:68
  38.7 3.5 %all-to-all-start = ((bf16[4,18,3584]{2,1,0:T(8,128)(2,1)}), bf16[4,18,3584]{2,1,0:T(8,128)(2,1)S(1)}, u32[]{:S(2)}, u32[]{:S(2)}) async-start(bf16[4,18,3584]{2,1,0:T(8,128)(2,1)} %reshape.80), calls=%async_computation | async-start | bytes 1376256 | tf_op jit(solution)/shard_map/all_to_all | solution.py:70
  42.2 0.0 copy-done.1
  42.2 10.5 %all-to-all-done = bf16[4,18,3584]{2,1,0:T(8,128)(2,1)S(1)} async-done(((bf16[4,18,3584]{2,1,0:T(8,128)(2,1)}), bf16[4,18,3584]{2,1,0:T(8,128)(2,1)S(1)}, u32[]{:S(2)}, u32[]{:S(2)}) %all-to-all-start) | async-done | bytes 516128 | tf_op jit(solution)/shard_map/all_to_all | solution.py:70
  52.8 1.4 %fusion = bf16[64,3584]{1,0:T(8,128)(2,1)} fusion(bf16[4,18,3584]{2,1,0:T(8,128)(2,1)S(1)} %all-to-all-done, f32[64]{0:T(128)S(1)} %bitcast_convert_fusion, pred[18,64]{1,0:T(8,128)(4,1)S(1)} %iota_compare_fusion.1, pred[4,64]{1,0:T(4,128)(4,1)S(1)} %convert_compare_fusion), kind=kOutput, calls=%fused_computation.4 | convolution fusion | flops 198419456 | bytes 976512 | tf_op jit(solution)/shard_map/ecf,ecd->fd/dot_general | solution.py:75
  (4 shorter events, 0.0 us)
Async XLA Ops:
  0.0 2.4 %copy-start = (bf16[64,3584]{1,0:T(8,128)(2,1)S(1)}, bf16[64,3584]{1,0:T(8,128)(2,1)}, u32[]{:S(2)}) copy-start(bf16[64,3584]{1,0:T(8,128)(2,1)} %param.6) | copy-start | bytes 1376260
  2.8 3.2 %collective-permute-start = (bf16[1,18,3584]{2,1,0:T(8,128)(2,1)S(1)}, bf16[1,18,3584]{2,1,0:T(8,128)(2,1)S(1)}, u32[]{:S(2)}, u32[]{:S(2)}) collective-permute-start(bf16[1,18,3584]{2,1,0:T(8,128)(2,1)S(1)} %get-tuple-element.8), channel_id=1, source_target_pairs={{0,8},{8,0},{16,24},{24,16},{1,9},{9,1},{17,25},{25,17},{2,10},{10... | collective-permute-start | bytes 387080 | tf_op jit(solution)/shard_map/ppermute | solution.py:33
  3.4 7.8 %collective-permute-start.1 = (bf16[1,18,3584]{2,1,0:T(8,128)(2,1)S(1)}, bf16[1,18,3584]{2,1,0:T(8,128)(2,1)S(1)}, u32[]{:S(2)}, u32[]{:S(2)}) collective-permute-start(bf16[1,18,3584]{2,1,0:T(8,128)(2,1)S(1)} %get-tuple-element.7), channel_id=1, source_target_pairs={{0,16},{8,24},{16,0},{24,8},{1,17},{9,25},{17,1},{25,9},{2,18},{10... | collective-permute-start | bytes 387080 | tf_op jit(solution)/shard_map/ppermute | solution.py:33
  6.0 8.4 %collective-permute-start.2 = (bf16[1,18,3584]{2,1,0:T(8,128)(2,1)S(1)}, bf16[1,18,3584]{2,1,0:T(8,128)(2,1)S(1)}, u32[]{:S(2)}, u32[]{:S(2)}) collective-permute-start(bf16[1,18,3584]{2,1,0:T(8,128)(2,1)S(1)} %get-tuple-element.6), channel_id=1, source_target_pairs={{0,24},{8,16},{16,8},{24,0},{1,25},{9,17},{17,9},{25,1},{2,26},{10... | collective-permute-start | bytes 387080 | tf_op jit(solution)/shard_map/ppermute | solution.py:33
  23.1 19.1 %copy-start.1 = (bf16[64,1]{0,1:T(2,128)(2,1)S(1)}, bf16[64,1]{0,1:T(2,128)(2,1)}, u32[]{:S(2)}) copy-start(bf16[64,1]{0,1:T(2,128)(2,1)} %param.8) | copy-start | bytes 388
  38.7 14.0 %all-to-all-start = ((bf16[4,18,3584]{2,1,0:T(8,128)(2,1)}), bf16[4,18,3584]{2,1,0:T(8,128)(2,1)S(1)}, u32[]{:S(2)}, u32[]{:S(2)}) async-start(bf16[4,18,3584]{2,1,0:T(8,128)(2,1)} %reshape.80), calls=%async_computation | async-start | bytes 1376256 | tf_op jit(solution)/shard_map/all_to_all | solution.py:70
